TPU v7x, 32 devices: a whole 2x2x4 slice. The times are simulated.
32 devices in a mesh: gx: 4 (over y, x), gz: 8 (over z, core).
Axes of the slice: x: 2, y: 2, z: 4, core: 2. Of those that a mesh axis runs over, the one named last changes fastest.
Arguments:
- pop_ratio: float32 [19, 16, 64, 512], P(None, None, 'gz', 'gx'), may hold values from 0.6 to 1.4
- solid_blocks: int32 [4, 16, 128], P(None, 'gz', 'gx'), may hold values 0 or 1
- shift_whole: int32 [2], replicated, may hold values from 0 to 511
- shift_frac: int32 [2], replicated, may hold values from 0 to 4095
Outputs:
- populations: float32 [19, 16, 64, 512], P(None, None, 'gz', 'gx')
- accumulated: float32 [2, 16, 64, 512], P(None, None, 'gz', 'gx')
- profiles: float32 [2, 16, 64], P(None, None, 'gz')
Inputs may be any that keep to these rules, and one draw needn't show every extreme that they name: `shift_whole`: whole cells of the displacement, below 512.
All inputs are finite; a program needn't handle non-finite values. No bound on the sum of `solid_blocks` on one device may be relied on, other than what follows from the above.
Results may differ from a plain program's by a relative error of at most 0.00023.
Values sent between devices are 32-bit elements; how exact they have to be, the bound alone decides.
No kernel may reach another device: no remote copies, remote signals or barrier semaphores. Data moves between devices by JAX's collectives and lax.ppermute only.
A program may use at most 64 MiB of HBM per device.

v0:
```python
import jax
import jax.numpy as jnp
import numpy as np
from jax import lax
from jax.sharding import PartitionSpec as P

STEPS = 2
BLOCK = 4
velocity_list = [
    (0, 0, 0),
    (1, 0, 0),
    (-1, 0, 0),
    (0, 1, 0),
    (0, -1, 0),
    (0, 0, 1),
    (0, 0, -1),
    (1, 1, 0),
    (-1, -1, 0),
    (1, -1, 0),
    (-1, 1, 0),
    (1, 0, 1),
    (-1, 0, -1),
    (1, 0, -1),
    (-1, 0, 1),
    (0, 1, 1),
    (0, -1, -1),
    (0, 1, -1),
    (0, -1, 1),
]
velocities = np.array(velocity_list)
lattice_weights = np.array([1.0 / 3.0] + [1.0 / 18.0] * 6 + [1.0 / 36.0] * 12)
opposite = np.array(
    [velocity_list.index((-entry[0], -entry[1], -entry[2])) for entry in velocity_list]
)
rising = [index for index in range(19) if velocities[index, 1] == 1]
falling = [index for index in range(19) if velocities[index, 1] == -1]
wall_speed = 0.08
visc_rate = 1.25
fraction_unit = 4096.0
relax_rates = np.array(
    [
        0.0,
        1.19,
        1.4,
        0.0,
        1.2,
        0.0,
        1.2,
        0.0,
        1.2,
        1.25,
        1.4,
        1.25,
        1.4,
        1.25,
        1.25,
        1.25,
        1.98,
        1.98,
        1.98,
    ]
)


def extended(value, sides, width):
    for axis, dim in sides:
        count, length = (lax.axis_size(axis), value.shape[dim])
        up = [(i, (i + 1) % count) for i in range(count)]
        down = [(j, i) for i, j in up]
        last = lax.slice_in_dim(value, length - width, length, axis=dim)
        initial = lax.slice_in_dim(value, 0, width, axis=dim)
        before = lax.ppermute(last, axis, up)
        after = lax.ppermute(initial, axis, down)
        value = jnp.concatenate([before, value, after], axis=dim)
    return value


def moment_rows():
    vel_x = velocities[:, 0] * 1.0
    vel_y = velocities[:, 1] * 1.0
    vel_z = velocities[:, 2] * 1.0
    speed_sq = vel_x * vel_x + vel_y * vel_y + vel_z * vel_z
    rows = [
        np.ones(19),
        19 * speed_sq - 30,
        (21 * speed_sq * speed_sq - 53 * speed_sq + 24) / 2,
        vel_x,
        (5 * speed_sq - 9) * vel_x,
        vel_y,
        (5 * speed_sq - 9) * vel_y,
        vel_z,
        (5 * speed_sq - 9) * vel_z,
        3 * vel_x * vel_x - speed_sq,
        (3 * speed_sq - 5) * (3 * vel_x * vel_x - speed_sq),
        vel_y * vel_y - vel_z * vel_z,
        (3 * speed_sq - 5) * (vel_y * vel_y - vel_z * vel_z),
        vel_x * vel_y,
        vel_y * vel_z,
        vel_x * vel_z,
        (vel_y * vel_y - vel_z * vel_z) * vel_x,
        (vel_z * vel_z - vel_x * vel_x) * vel_y,
        (vel_x * vel_x - vel_y * vel_y) * vel_z,
    ]
    return np.stack(rows)


def relax_matrix():
    moments = moment_rows()
    scaled = moments.T / np.sum(moments * moments, axis=1)
    return (scaled @ (relax_rates[:, None] * moments)).astype(np.float32)


def column(values):
    return jnp.asarray(np.asarray(values, dtype=np.float32).reshape(-1, 1, 1, 1))


def plane_column(values):
    return jnp.asarray(np.asarray(values, dtype=np.float32).reshape(-1, 1, 1))


def expand(blocks):
    deep, tall, wide = blocks.shape
    big = jnp.broadcast_to(
        blocks[:, None, :, None, :, None], (deep, BLOCK, tall, BLOCK, wide, BLOCK)
    )
    return big.reshape(deep * BLOCK, tall * BLOCK, wide * BLOCK).astype(jnp.float32)


def collide(popul, solid):
    rho = jnp.sum(popul, axis=0)
    mom_x = jnp.sum(column(velocities[:, 0]) * popul, axis=0)
    mom_y = jnp.sum(column(velocities[:, 1]) * popul, axis=0)
    mom_z = jnp.sum(column(velocities[:, 2]) * popul, axis=0)
    inverse = 1.0 / rho
    vel_x = mom_x * inverse
    vel_y = mom_y * inverse
    vel_z = mom_z * inverse
    along = (
        column(velocities[:, 0]) * vel_x
        + column(velocities[:, 1]) * vel_y
        + column(velocities[:, 2]) * vel_z
    )
    speed_sq = vel_x * vel_x + vel_y * vel_y + vel_z * vel_z
    equil = (
        column(lattice_weights) * rho * (1.0 + 3.0 * along + 4.5 * along * along - 1.5 * speed_sq)
    )
    noneq = popul - equil
    relaxed = jnp.dot(
        jnp.asarray(relax_matrix()), noneq.reshape(19, -1), precision=lax.Precision.HIGHEST
    ).reshape(popul.shape)
    post = jnp.where(solid > 0, popul[opposite], popul - relaxed)
    fluid = 1.0 - solid
    stress = -(1.0 - 0.5 * visc_rate) * jnp.sum(
        column(velocities[:, 0] * velocities[:, 1]) * noneq, axis=0
    )
    return (post, jnp.stack([fluid * mom_x, fluid * stress]))


def assemble(shifted, le_top, le_bot):
    pieces = []
    for index in range(19):
        lift = velocities[index, 1]
        if lift == 0:
            pieces.append(shifted[index])
        elif lift > 0:
            pieces.append(
                jnp.concatenate([le_top[rising.index(index)][None], shifted[index, :-1]], axis=0)
            )
        else:
            pieces.append(
                jnp.concatenate([shifted[index, 1:], le_bot[falling.index(index)][None]], axis=0)
            )
    return jnp.stack(pieces)


def stream_across(post):
    depth_z = post.shape[2]
    width_x = post.shape[3]
    padded = extended(post, (("gx", 3), ("gz", 2)), 1)
    pieces = []
    for index in range(19):
        start_z = 1 - int(velocities[index, 2])
        start_x = 1 - int(velocities[index, 0])
        pieces.append(padded[index, :, start_z : start_z + depth_z, start_x : start_x + width_x])
    return jnp.stack(pieces)


def displaced_windows(planes, whole):
    width_x = planes.shape[3]
    count = lax.axis_size("gx")
    total = count * width_x
    offset_top = whole % total
    offset_bot = (total - whole - 1) % total
    full = lax.all_gather(planes, "gx", axis=3, tiled=True)
    doubled = jnp.concatenate([full, full[:, :, :, : width_x + 1]], axis=3)
    anchor = lax.axis_index("gx") * width_x
    start_top = (anchor + offset_top) % total
    start_bot = (anchor + offset_bot) % total
    win_top = lax.dynamic_slice_in_dim(doubled[0], start_top, width_x + 1, 2)
    win_bot = lax.dynamic_slice_in_dim(doubled[1], start_bot, width_x + 1, 2)
    return (win_top, win_bot)


def local(pop_ratio, solid_blocks, shift_whole, shift_frac):
    popul = pop_ratio * column(lattice_weights)
    solid = expand(solid_blocks)
    width_x = popul.shape[3]
    planes_y = popul.shape[1]
    accumulated = jnp.zeros((2,) + popul.shape[1:], jnp.float32)
    top_fix = plane_column(6.0 * lattice_weights[rising] * velocities[rising, 0] * wall_speed)
    bot_fix = plane_column(6.0 * lattice_weights[falling] * velocities[falling, 0] * wall_speed)
    for step in range(STEPS):
        post, fields = collide(popul, solid)
        accumulated = accumulated + fields
        shifted = stream_across(post)
        whole = shift_whole[step]
        weight = shift_frac[step].astype(jnp.float32) / fraction_unit
        planes = jnp.stack([shifted[np.array(rising), planes_y - 1], shifted[np.array(falling), 0]])
        win_top, win_bot = displaced_windows(planes, whole)
        le_top = (1.0 - weight) * win_top[:, :, :width_x] + weight * win_top[:, :, 1:] - top_fix
        le_bot = (1.0 - weight) * win_bot[:, :, 1:] + weight * win_bot[:, :, :width_x] + bot_fix
        popul = assemble(shifted, le_top, le_bot)
    profiles = lax.psum(jnp.sum(accumulated, axis=3), "gx")
    return (popul, accumulated, profiles)


def solution(mesh):
    return jax.shard_map(
        local,
        mesh=mesh,
        in_specs=(P(None, None, "gz", "gx"), P(None, "gz", "gx"), P(), P()),
        out_specs=(P(None, None, "gz", "gx"), P(None, None, "gz", "gx"), P(None, None, "gz")),
        check_vma=False,
    )
```

profile of v0, /device:TPU:0, one launch (start us, length us, event | category | flops | bytes accessed | tf_op | source)
XLA Modules:
  0.0 189.6 jit_solution(16554818729477392936)
XLA Ops:
  0.7 0.8 pad_clamp_fusion
  1.5 1.9 %multiply_reduce_fusion.6 = (f32[16,8,128]{2,1,0:T(8,128)S(1)}, f32[16,8,128]{2,1,0:T(8,128)S(1)}, f32[16,8,128]{2,1,0:T(8,128)S(1)}, f32[16,8,128]{2,1,0:T(8,128)S(1)}) fusion(f32[19]{0:T(128)} %constant.136, f32[19,16,8,128]{3,2,1,0:T(8,128)} %param.36, f32[19]{0:T(128)} %constant.134, f32[19]{0:T(128)} %constant.137, f32[19]{0:T(128)} %constant.138), kind=kLoop, calls=%fused_computation.42 | loop fusion | flops 2424832 | bytes 1507632 | tf_op jit(solution)/shard_map/reduce_sum | solution.py:131
  4.0 2.2 %fusion.17 = (f32[19,16,8,128]{3,2,1,0:T(8,128)S(1)}, f32[19,16,8,128]{3,2,1,0:T(8,128)}) fusion(f32[16,8,128]{2,1,0:T(8,128)S(1)} %get-tuple-element.47, f32[16,8,128]{2,1,0:T(8,128)S(1)} %get-tuple-element.50, f32[19]{0:T(128)S(1)} %copy-done.68, f32[16,8,128]{2,1,0:T(8,128)S(1)} %get-tuple-element.49, f32[19]{0:T(128)S(1)} %copy-done.65, ...), kind=kLoop, calls=%fused_computation.25 | loop fusion | flops 4669440 | bytes 4063536 | tf_op jit(solution)/shard_map/sub | solution.py:147
  6.4 0.9 copy-done.8
  7.3 0.9 copy.52
  8.2 1.4 fusion.92
  9.6 1.4 copy.53
  11.3 1.8 gt.9
  13.1 1.7 gather_fusion
  14.8 1.9 fusion.25
  16.6 1.5 fusion.85
  18.1 2.2 %copy.39 = f32[19,16,8,1]{0,2,3,1:T(8,128)S(1)} copy(f32[19,16,8,1]{3,2,1,0:T(8,128)} %get-tuple-element.90) | data formatting | bytes 19456 | tf_op jit(solution)/shard_map/slice | solution.py:70
  20.3 3.0 %collective-permute-start = (f32[19,16,8,1]{0,2,3,1:T(8,128)S(1)}, f32[19,16,8,1]{0,2,3,1:T(8,128)S(1)}, u32[]{:S(2)}, u32[]{:S(2)}) collective-permute-start(f32[19,16,8,1]{0,2,3,1:T(8,128)S(1)} %copy.39), channel_id=1, source_target_pairs={{0,8},{8,16},{16,24},{24,0},{1,9},{9,17},{17,25},{25,1},{2,10},{10... | collective-permute-start | bytes 29192 | tf_op jit(solution)/shard_map/ppermute | solution.py:72
  23.3 1.6 copy.41
  24.9 1.0 collective-permute-start.1
  33.8 2.3 %sub.117 = f32[1,16,8,128]{3,2,1,0:T(8,128)} reshape(f32[4,4,2,4,32,4]{5,4,3,2,1,0:T(8,128)S(1)} %broadcast_in_dim.49) | data formatting | bytes 131072 | tf_op jit(solution)/shard_map/sub | solution.py:152
  36.7 1.3 copy.40
  38.0 3.1 %copy.42 = f32[19,16,8,1]{3,2,1,0:T(8,128)} copy(f32[19,16,8,1]{0,2,3,1:T(8,128)} %collective-permute-done.1) | data formatting | bytes 19456 | tf_op jit(solution)/shard_map/ppermute | solution.py:73
  41.1 1.8 fusion.50
  42.8 2.0 %pad_maximum_fusion.3 = (f32[19,16,1,130]{3,2,1,0:T(1,128)S(1)}, f32[19,16,1,130]{3,2,1,0:T(1,128)S(1)}) fusion(f32[19,16,8,1]{3,2,1,0:T(8,128)S(1)} %copy-done.2, f32[19,16,8,128]{3,2,1,0:T(8,128)S(1)} %fusion.25, f32[19,16,8,1]{3,2,1,0:T(8,128)S(1)} %copy.40), kind=kLoop, calls=%fused_computation.59 | loop fusion | flops 158080 | bytes 1580800 | tf_op jit(solution)/shard_map/concatenate | solution.py:74
  44.8 0.7 constant_dynamic-update-slice_fusion.34
  45.6 0.8 constant_dynamic-update-slice_fusion.33
  46.3 2.5 %copy.71 = f32[19,16,8,128]{3,2,1,0:T(8,128)} copy(f32[19,16,8,128]{3,2,1,0:T(8,128)} %get-tuple-element.43) | data formatting | bytes 2490368
  48.8 3.5 %collective-permute-start.3 = (f32[19,16,1,130]{3,2,1,0:T(1,128)S(1)}, f32[19,16,1,130]{3,2,1,0:T(1,128)S(1)}, u32[]{:S(2)}, u32[]{:S(2)}) collective-permute-start(f32[19,16,1,130]{3,2,1,0:T(1,128)S(1)} %get-tuple-element.65), channel_id=1, source_target_pairs={{1,0},{2,1},{3,2},{4,3},{5,4},{6,5},{7,6},{0,7},{9,8},{10,9},{11,1... | collective-permute-start | bytes 474248 | tf_op jit(solution)/shard_map/ppermute | solution.py:73
  53.0 4.7 %collective-permute-done.2 = f32[19,16,1,130]{3,2,1,0:T(1,128)S(1)} collective-permute-done((f32[19,16,1,130]{3,2,1,0:T(1,128)S(1)}, f32[19,16,1,130]{3,2,1,0:T(1,128)S(1)}, u32[]{:S(2)}, u32[]{:S(2)}) %collective-permute-start.2) | collective-permute-done | bytes 158112 | tf_op jit(solution)/shard_map/ppermute | solution.py:72
  58.4 0.7 constant_dynamic-update-slice_fusion.11
  62.8 0.8 constant_dynamic-update-slice_fusion.5
  64.3 0.8 constant_dynamic-update-slice_fusion.3
  65.8 0.8 constant_dynamic-update-slice_fusion.1
  67.3 1.9 gather_fusion.2
  69.2 2.5 %gather_fusion.1 = f32[5,8,128]{2,1,0:T(8,128)} fusion(f32[19,16,8,128]{3,2,1,0:T(8,128)} %constant_dynamic-update-slice_fusion, s32[5]{0:T(128)S(1)} %copy-done.47), kind=kCustom, calls=%fused_computation.1 | custom fusion | bytes 41000 | tf_op jit(solution)/shard_map/gather | solution.py:218
  71.7 0.8 pad_maximum_fusion.48
  72.5 10.9 %all_gather.6 = f32[2,5,8,512]{3,2,1,0:T(8,128)S(1)} all-gather(f32[2,5,8,128]{3,2,1,0:T(8,128)S(1)} %pad_maximum_fusion.48), channel_id=1, replica_groups=mesh['gx'=4,'gz'=8] {'gx'}, dimensions={3}, use_global_device_ids=true | all-gather | bytes 204800 | tf_op jit(solution)/shard_map/all_gather | solution.py:194
  85.6 1.1 copy-done.4
  87.0 1.0 copy-done.5
  88.0 1.0 multiply_reduce_fusion.1
  89.1 2.2 %gather_fusion.3 = f32[19,16,8,128]{3,2,1,0:T(8,128)S(1)} fusion(f32[19,16,8,128]{3,2,1,0:T(8,128)} %copy-done.5, s32[1024]{0:T(1024)} %copy-done.71), kind=kCustom, calls=%fused_computation.3 | custom fusion | bytes 2490444 | tf_op jit(solution)/shard_map/gather | solution.py:151
  92.1 1.4 pad_maximum_fusion.23
  93.5 1.3 pad_maximum_fusion.25
  96.2 0.8 fusion.69
  97.7 6.3 %stack.178 = f32[19,16384]{1,0:T(8,128)} concatenate(f32[1,16384]{1,0:T(1,128)} %bitcast.276, f32[1,16384]{1,0:T(1,128)} %bitcast.272, f32[1,16384]{1,0:T(1,128)} %bitcast.273, f32[1,16384]{1,0:T(1,128)} %bitcast.277, f32[1,16384]{1,0:T(1,128)} %bitcast.279, f32[1,16384]{1,0:T(1,128)S(1)} %bitcast.264, f32[1,16384]{1,0:T(1,128)S(1)} %bitcast.265, f32[1,16384]{1,0:T(1,128)} %bitcast.278, ...), dimensions={0} | concatenate | bytes 2490368 | tf_op jit(solution)/shard_map/stack | solution.py:173
  104.1 3.5 %fusion.4 = f32[19,16384]{1,0:T(8,128)S(1)} fusion(f32[19,19]{1,0:T(8,128)S(1)} %copy-done.59, f32[19,16384]{1,0:T(8,128)} %stack.178, f32[16384]{0:T(1024)S(1)} %bitcast.274, f32[16384]{0:T(1024)S(1)} %get-tuple-element.93, f32[19]{0:T(128)S(1)} %copy-done.70, f32[16384]{0:T(1024)S(1)} %get-tuple-element.96, f32[19]{0:T(128)S(1)} %copy-done.67, ...), kind=kOutput, calls=%fused_computation.13 | convolution fusion | flops 75333632 | bytes 2819796 | tf_op jit(solution)/shard_map/dot_general | solution.py:148
  107.9 1.0 copy-done.6
  109.2 1.3 fusion.23
  110.5 1.5 fusion.83
  112.0 2.2 %copy.47 = f32[19,16,8,1]{0,2,3,1:T(8,128)S(1)} copy(f32[19,16,8,1]{3,2,1,0:T(8,128)} %get-tuple-element.82) | data formatting | bytes 19456 | tf_op jit(solution)/shard_map/slice | solution.py:71
  114.2 1.5 collective-permute-start.5
  115.7 1.0 copy.45
  117.9 16.0 %psum.7 = f32[2,16,8]{2,1,0:T(8,128)S(1)} all-reduce(f32[2,16,8]{2,1,0:T(8,128)S(1)} %get-tuple-element.15), channel_id=1, replica_groups=mesh['gx'=4,'gz'=8] {'gx'}, use_global_device_ids=true, to_apply=%region_10.11 | all-reduce | flops 256 | bytes 2048 | tf_op jit(solution)/shard_map/psum | solution.py:223
  134.6 1.3 copy.48
  135.9 2.2 %copy.46 = f32[19,16,8,1]{3,2,1,0:T(8,128)} copy(f32[19,16,8,1]{0,2,3,1:T(8,128)S(1)} %collective-permute-done.4) | data formatting | bytes 19456 | tf_op jit(solution)/shard_map/ppermute | solution.py:72
  138.1 1.6 pad_maximum_fusion.12
  139.7 0.8 fusion.46
  140.5 2.0 %pad_maximum_fusion = (f32[19,16,1,130]{3,2,1,0:T(1,128)S(1)}, f32[19,16,1,130]{3,2,1,0:T(1,128)S(1)}) fusion(f32[19,16,8,1]{3,2,1,0:T(8,128)S(1)} %copy.48, f32[19,16,8,128]{3,2,1,0:T(8,128)S(1)} %get-tuple-element.75, f32[19,16,8,1]{3,2,1,0:T(8,128)S(1)} %copy-done), kind=kLoop, calls=%fused_computation.56 | loop fusion | flops 158080 | bytes 1580800 | tf_op jit(solution)/shard_map/concatenate | solution.py:74
  143.8 2.4 %copy.103 = f32[19,16,8,128]{3,2,1,0:T(8,128)} copy(f32[19,16,8,128]{3,2,1,0:T(8,128)} %constant_dynamic-update-slice_fusion.69) | data formatting | bytes 2490368
  146.2 3.5 %collective-permute-start.7 = (f32[19,16,1,130]{3,2,1,0:T(1,128)S(1)}, f32[19,16,1,130]{3,2,1,0:T(1,128)S(1)}, u32[]{:S(2)}, u32[]{:S(2)}) collective-permute-start(f32[19,16,1,130]{3,2,1,0:T(1,128)S(1)} %get-tuple-element.61), channel_id=1, source_target_pairs={{1,0},{2,1},{3,2},{4,3},{5,4},{6,5},{7,6},{0,7},{9,8},{10,9},{11,1... | collective-permute-start | bytes 474248 | tf_op jit(solution)/shard_map/ppermute | solution.py:73
  150.4 5.4 %collective-permute-done.6 = f32[19,16,1,130]{3,2,1,0:T(1,128)S(1)} collective-permute-done((f32[19,16,1,130]{3,2,1,0:T(1,128)S(1)}, f32[19,16,1,130]{3,2,1,0:T(1,128)S(1)}, u32[]{:S(2)}, u32[]{:S(2)}) %collective-permute-start.6) | collective-permute-done | bytes 158112 | tf_op jit(solution)/shard_map/ppermute | solution.py:72
  160.8 0.7 constant_dynamic-update-slice_fusion.41
  162.3 0.8 constant_dynamic-update-slice_fusion.39
  163.7 0.8 constant_dynamic-update-slice_fusion.37
  165.3 1.9 gather_fusion.5
  167.1 2.5 %gather_fusion.4 = f32[5,8,128]{2,1,0:T(8,128)} fusion(f32[19,16,8,128]{3,2,1,0:T(8,128)} %constant_dynamic-update-slice_fusion.36, s32[5]{0:T(128)S(1)} %copy-done.47), kind=kCustom, calls=%fused_computation.4 | custom fusion | bytes 41000 | tf_op jit(solution)/shard_map/gather | solution.py:218
  169.6 0.8 pad_maximum_fusion.49
  170.4 8.3 %all_gather.7 = f32[2,5,8,512]{3,2,1,0:T(8,128)S(1)} all-gather(f32[2,5,8,128]{3,2,1,0:T(8,128)S(1)} %pad_maximum_fusion.49), channel_id=1, replica_groups=mesh['gx'=4,'gz'=8] {'gx'}, dimensions={3}, use_global_device_ids=true | all-gather | bytes 204800 | tf_op jit(solution)/shard_map/all_gather | solution.py:194
  (253 shorter events, 37.7 us)
Async XLA Ops:
  0.6 3.4 %copy-start.60 = (f32[19]{0:T(128)S(1)}, f32[19]{0:T(128)}, u32[]{:S(2)}) copy-start(f32[19]{0:T(128)} %constant.136) | copy-start | bytes 232
  0.6 3.4 %copy-start.63 = (f32[19]{0:T(128)S(1)}, f32[19]{0:T(128)}, u32[]{:S(2)}) copy-start(f32[19]{0:T(128)} %constant.134) | copy-start | bytes 232
  0.7 3.4 %copy-start.65 = (f32[19]{0:T(128)S(1)}, f32[19]{0:T(128)}, u32[]{:S(2)}) copy-start(f32[19]{0:T(128)} %constant.137) | copy-start | bytes 232
  0.7 3.4 %copy-start.68 = (f32[19]{0:T(128)S(1)}, f32[19]{0:T(128)}, u32[]{:S(2)}) copy-start(f32[19]{0:T(128)} %constant.138) | copy-start | bytes 232
  0.7 3.3 %copy-start.7 = (f32[19,16,8,128]{3,2,1,0:T(8,128)S(1)}, f32[19,16,8,128]{3,2,1,0:T(8,128)}, u32[]{:S(2)}) copy-start(f32[19,16,8,128]{3,2,1,0:T(8,128)} %param.36) | copy-start | bytes 3735556
  1.5 11.6 %copy-start.71 = (s32[1024]{0:T(1024)}, s32[1024]{0:T(1024)S(1)}, u32[]{:S(2)}) copy-start(s32[1024]{0:T(1024)S(1)} %pad_clamp_fusion) | copy-start | bytes 12292
  9.6 3.5 %copy-start.10 = (f32[19,16,8,128]{3,2,1,0:T(8,128)S(1)}, f32[19,16,8,128]{3,2,1,0:T(8,128)}, u32[]{:S(2)}) copy-start(f32[19,16,8,128]{3,2,1,0:T(8,128)} %get-tuple-element.74) | copy-start | bytes 3735556
  18.1 8.4 %copy-start.75 = (s32[2]{0:T(128)S(1)}, s32[2]{0:T(128)}, u32[]{:S(2)}) copy-start(s32[2]{0:T(128)} %param.38) | copy-start | bytes 28
  18.1 9.0 %copy-start.76 = (s32[2]{0:T(128)S(1)}, s32[2]{0:T(128)}, u32[]{:S(2)}) copy-start(s32[2]{0:T(128)} %param.39) | copy-start | bytes 28
  20.3 16.4 %collective-permute-start = (f32[19,16,8,1]{0,2,3,1:T(8,128)S(1)}, f32[19,16,8,1]{0,2,3,1:T(8,128)S(1)}, u32[]{:S(2)}, u32[]{:S(2)}) collective-permute-start(f32[19,16,8,1]{0,2,3,1:T(8,128)S(1)} %copy.39), channel_id=1, source_target_pairs={{0,8},{8,16},{16,24},{24,0},{1,9},{9,17},{17,25},{25,1},{2,10},{10... | collective-permute-start | bytes 29192 | tf_op jit(solution)/shard_map/ppermute | solution.py:72
  24.9 13.1 %collective-permute-start.1 = (f32[19,16,8,1]{0,2,3,1:T(8,128)}, f32[19,16,8,1]{0,2,3,1:T(8,128)}, u32[]{:S(2)}, u32[]{:S(2)}) collective-permute-start(f32[19,16,8,1]{0,2,3,1:T(8,128)} %copy.41), channel_id=1, source_target_pairs={{8,0},{16,8},{24,16},{0,24},{9,1},{17,9},{25,17},{1,25},{10,2},{18... | collective-permute-start | bytes 29192 | tf_op jit(solution)/shard_map/ppermute | solution.py:73
  41.1 1.8 copy-start.2
  48.8 8.9 %collective-permute-start.2 = (f32[19,16,1,130]{3,2,1,0:T(1,128)S(1)}, f32[19,16,1,130]{3,2,1,0:T(1,128)S(1)}, u32[]{:S(2)}, u32[]{:S(2)}) collective-permute-start(f32[19,16,1,130]{3,2,1,0:T(1,128)S(1)} %get-tuple-element.66), channel_id=1, source_target_pairs={{0,1},{1,2},{2,3},{3,4},{4,5},{5,6},{6,7},{7,0},{8,9},{9,10},{10,1... | collective-permute-start | bytes 474248 | tf_op jit(solution)/shard_map/ppermute | solution.py:72
  48.8 9.6 %collective-permute-start.3 = (f32[19,16,1,130]{3,2,1,0:T(1,128)S(1)}, f32[19,16,1,130]{3,2,1,0:T(1,128)S(1)}, u32[]{:S(2)}, u32[]{:S(2)}) collective-permute-start(f32[19,16,1,130]{3,2,1,0:T(1,128)S(1)} %get-tuple-element.65), channel_id=1, source_target_pairs={{1,0},{2,1},{3,2},{4,3},{5,4},{6,5},{7,6},{0,7},{9,8},{10,9},{11,1... | collective-permute-start | bytes 474248 | tf_op jit(solution)/shard_map/ppermute | solution.py:73
  66.6 2.6 %copy-start.47 = (s32[5]{0:T(128)S(1)}, s32[5]{0:T(128)}, u32[]{:S(2)}) copy-start(s32[5]{0:T(128)} %constant.208) | copy-start | bytes 64
  67.3 17.1 %copy-start.72 = (f32[5]{0:T(128)S(1)}, f32[5]{0:T(128)}, u32[]{:S(2)}) copy-start(f32[5]{0:T(128)} %constant.144) | copy-start | bytes 64
  71.7 12.9 %copy-start.17 = (f32[15,8,128]{2,1,0:T(8,128)S(1)}, f32[15,8,128]{2,1,0:T(8,128)}, u32[]{:S(2)}) copy-start(f32[15,8,128]{2,1,0:T(8,128)} %get-tuple-element.88) | copy-start | bytes 184324
  71.7 13.5 %copy-start.3 = (f32[19,16,8,1]{3,2,1,0:T(8,128)S(1)}, f32[19,16,8,1]{3,2,1,0:T(8,128)}, u32[]{:S(2)}) copy-start(f32[19,16,8,1]{3,2,1,0:T(8,128)} %copy.42) | copy-start | bytes 29188
  84.6 2.2 %copy-start.53 = (f32[1,8,128]{2,1,0:T(8,128)}, f32[1,8,128]{2,1,0:T(8,128)S(1)}, u32[]{:S(2)}) copy-start(f32[1,8,128]{2,1,0:T(8,128)S(1)} %get-tuple-element.114) | copy-start | bytes 12292
  84.6 2.2 %copy-start.51 = (f32[1,8,128]{2,1,0:T(8,128)}, f32[1,8,128]{2,1,0:T(8,128)S(1)}, u32[]{:S(2)}) copy-start(f32[1,8,128]{2,1,0:T(8,128)S(1)} %get-tuple-element.113) | copy-start | bytes 12292
  84.6 2.3 %copy-start.49 = (f32[1,8,128]{2,1,0:T(8,128)}, f32[1,8,128]{2,1,0:T(8,128)S(1)}, u32[]{:S(2)}) copy-start(f32[1,8,128]{2,1,0:T(8,128)S(1)} %get-tuple-element.112) | copy-start | bytes 12292
  85.5 2.5 %copy-start.61 = (f32[19]{0:T(128)S(1)}, f32[19]{0:T(128)}, u32[]{:S(2)}) copy-start(f32[19]{0:T(128)} %constant.136) | copy-start | bytes 232
  85.5 2.5 %copy-start.66 = (f32[19]{0:T(128)S(1)}, f32[19]{0:T(128)}, u32[]{:S(2)}) copy-start(f32[19]{0:T(128)} %constant.137) | copy-start | bytes 232
  85.5 2.5 %copy-start.69 = (f32[19]{0:T(128)S(1)}, f32[19]{0:T(128)}, u32[]{:S(2)}) copy-start(f32[19]{0:T(128)} %constant.138) | copy-start | bytes 232
  89.0 2.3 %copy-start.16 = (f32[15,8,128]{2,1,0:T(8,128)S(1)}, f32[15,8,128]{2,1,0:T(8,128)}, u32[]{:S(2)}) copy-start(f32[15,8,128]{2,1,0:T(8,128)} %get-tuple-element.87) | copy-start | bytes 184324
  89.0 2.3 %copy-start.18 = (f32[15,8,128]{2,1,0:T(8,128)S(1)}, f32[15,8,128]{2,1,0:T(8,128)}, u32[]{:S(2)}) copy-start(f32[15,8,128]{2,1,0:T(8,128)} %get-tuple-element.88) | copy-start | bytes 184324
  89.0 3.0 %copy-start.28 = (f32[15,8,128]{2,1,0:T(8,128)S(1)}, f32[15,8,128]{2,1,0:T(8,128)}, u32[]{:S(2)}) copy-start(f32[15,8,128]{2,1,0:T(8,128)} %copy-done.27) | copy-start | bytes 184324
  89.1 3.0 %copy-start.30 = (f32[15,8,128]{2,1,0:T(8,128)S(1)}, f32[15,8,128]{2,1,0:T(8,128)}, u32[]{:S(2)}) copy-start(f32[15,8,128]{2,1,0:T(8,128)} %copy-done.29) | copy-start | bytes 184324
  89.1 3.0 %copy-start.52 = (f32[1,8,128]{2,1,0:T(8,128)S(1)}, f32[1,8,128]{2,1,0:T(8,128)}, u32[]{:S(2)}) copy-start(f32[1,8,128]{2,1,0:T(8,128)} %copy-done.51) | copy-start | bytes 12292
  89.1 4.4 %copy-start.12 = (f32[15,8,128]{2,1,0:T(8,128)S(1)}, f32[15,8,128]{2,1,0:T(8,128)}, u32[]{:S(2)}) copy-start(f32[15,8,128]{2,1,0:T(8,128)} %get-tuple-element.71) | copy-start | bytes 184324
  89.1 4.4 %copy-start.14 = (f32[15,8,128]{2,1,0:T(8,128)S(1)}, f32[15,8,128]{2,1,0:T(8,128)}, u32[]{:S(2)}) copy-start(f32[15,8,128]{2,1,0:T(8,128)} %get-tuple-element.72) | copy-start | bytes 184324
  89.1 5.7 %copy-start.22 = (f32[15,8,128]{2,1,0:T(8,128)S(1)}, f32[15,8,128]{2,1,0:T(8,128)}, u32[]{:S(2)}) copy-start(f32[15,8,128]{2,1,0:T(8,128)} %copy-done.21) | copy-start | bytes 184324
  89.1 5.7 %copy-start.26 = (f32[15,8,128]{2,1,0:T(8,128)S(1)}, f32[15,8,128]{2,1,0:T(8,128)}, u32[]{:S(2)}) copy-start(f32[15,8,128]{2,1,0:T(8,128)} %copy-done.25) | copy-start | bytes 184324
  89.1 6.4 %copy-start.20 = (f32[15,8,128]{2,1,0:T(8,128)S(1)}, f32[15,8,128]{2,1,0:T(8,128)}, u32[]{:S(2)}) copy-start(f32[15,8,128]{2,1,0:T(8,128)} %copy-done.19) | copy-start | bytes 184324
  89.1 6.4 %copy-start.24 = (f32[15,8,128]{2,1,0:T(8,128)S(1)}, f32[15,8,128]{2,1,0:T(8,128)}, u32[]{:S(2)}) copy-start(f32[15,8,128]{2,1,0:T(8,128)} %copy-done.23) | copy-start | bytes 184324
  89.1 6.4 %copy-start.50 = (f32[1,8,128]{2,1,0:T(8,128)S(1)}, f32[1,8,128]{2,1,0:T(8,128)}, u32[]{:S(2)}) copy-start(f32[1,8,128]{2,1,0:T(8,128)} %copy-done.49) | copy-start | bytes 12292
  91.3 4.8 %copy-start.35 = (f32[16,8,128]{2,1,0:T(8,128)S(1)}, f32[16,8,128]{2,1,0:T(8,128)}, u32[]{:S(2)}) copy-start(f32[16,8,128]{2,1,0:T(8,128)} %get-tuple-element.12) | copy-start | bytes 196612
  91.3 4.8 %copy-start.38 = (f32[1,16,8,128]{3,2,1,0:T(8,128)S(1)}, f32[1,16,8,128]{3,2,1,0:T(8,128)}, u32[]{:S(2)}) copy-start(f32[1,16,8,128]{3,2,1,0:T(8,128)} %get-tuple-element.46) | copy-start | bytes 196612
  91.3 4.8 %copy-start.39 = (f32[1,16,8,128]{3,2,1,0:T(8,128)S(1)}, f32[1,16,8,128]{3,2,1,0:T(8,128)}, u32[]{:S(2)}) copy-start(f32[1,16,8,128]{3,2,1,0:T(8,128)} %get-tuple-element.44) | copy-start | bytes 196612
  91.4 4.8 %copy-start.54 = (f32[1,8,128]{2,1,0:T(8,128)S(1)}, f32[1,8,128]{2,1,0:T(8,128)}, u32[]{:S(2)}) copy-start(f32[1,8,128]{2,1,0:T(8,128)} %copy-done.53) | copy-start | bytes 12292
  91.4 4.8 %copy-start.56 = (f32[1,8,128]{2,1,0:T(8,128)S(1)}, f32[1,8,128]{2,1,0:T(8,128)}, u32[]{:S(2)}) copy-start(f32[1,8,128]{2,1,0:T(8,128)} %copy-done.55) | copy-start | bytes 12292
  92.0 5.5 %copy-start.33 = (f32[1,16,8,128]{3,2,1,0:T(8,128)S(1)}, f32[1,16,8,128]{3,2,1,0:T(8,128)}, u32[]{:S(2)}) copy-start(f32[1,16,8,128]{3,2,1,0:T(8,128)} %sub.117) | copy-start | bytes 196612
  92.1 5.5 %copy-start.37 = (f32[16,8,128]{2,1,0:T(8,128)S(1)}, f32[16,8,128]{2,1,0:T(8,128)}, u32[]{:S(2)}) copy-start(f32[16,8,128]{2,1,0:T(8,128)} %copy-done.36) | copy-start | bytes 196612
  92.1 5.5 %copy-start.41 = (f32[16,8,128]{2,1,0:T(8,128)S(1)}, f32[16,8,128]{2,1,0:T(8,128)}, u32[]{:S(2)}) copy-start(f32[16,8,128]{2,1,0:T(8,128)} %get-tuple-element.10) | copy-start | bytes 196612
  92.1 5.5 %copy-start.42 = (f32[16,8,128]{2,1,0:T(8,128)S(1)}, f32[16,8,128]{2,1,0:T(8,128)}, u32[]{:S(2)}) copy-start(f32[16,8,128]{2,1,0:T(8,128)} %get-tuple-element.11) | copy-start | bytes 196612
  97.6 6.4 %copy-start.32 = (f32[1,16,8,128]{3,2,1,0:T(8,128)S(1)}, f32[1,16,8,128]{3,2,1,0:T(8,128)}, u32[]{:S(2)}) copy-start(f32[1,16,8,128]{3,2,1,0:T(8,128)} %copy-done.31) | copy-start | bytes 196612
  97.6 6.4 %copy-start.59 = (f32[19,19]{1,0:T(8,128)S(1)}, f32[19,19]{1,0:T(8,128)}, u32[]{:S(2)}) copy-start(f32[19,19]{1,0:T(8,128)} %constant.119.clone) | copy-start | bytes 4336
  97.6 6.4 %copy-start.62 = (f32[19]{0:T(128)S(1)}, f32[19]{0:T(128)}, u32[]{:S(2)}) copy-start(f32[19]{0:T(128)} %constant.136) | copy-start | bytes 232
  97.6 6.4 %copy-start.64 = (f32[19]{0:T(128)S(1)}, f32[19]{0:T(128)}, u32[]{:S(2)}) copy-start(f32[19]{0:T(128)} %constant.134) | copy-start | bytes 232
  97.7 6.4 %copy-start.67 = (f32[19]{0:T(128)S(1)}, f32[19]{0:T(128)}, u32[]{:S(2)}) copy-start(f32[19]{0:T(128)} %constant.137) | copy-start | bytes 232
  97.7 6.4 %copy-start.70 = (f32[19]{0:T(128)S(1)}, f32[19]{0:T(128)}, u32[]{:S(2)}) copy-start(f32[19]{0:T(128)} %constant.138) | copy-start | bytes 232
  107.6 1.7 copy-start.9
  112.0 5.2 %copy-start.34 = (f32[1,16,8,128]{3,2,1,0:T(8,128)S(1)}, f32[1,16,8,128]{3,2,1,0:T(8,128)}, u32[]{:S(2)}) copy-start(f32[1,16,8,128]{3,2,1,0:T(8,128)} %sub.117) | copy-start | bytes 196612
  114.2 20.4 %collective-permute-start.5 = (f32[19,16,8,1]{0,2,3,1:T(8,128)S(1)}, f32[19,16,8,1]{0,2,3,1:T(8,128)S(1)}, u32[]{:S(2)}, u32[]{:S(2)}) collective-permute-start(f32[19,16,8,1]{0,2,3,1:T(8,128)S(1)} %copy.47), channel_id=1, source_target_pairs={{8,0},{16,8},{24,16},{0,24},{9,1},{17,9},{25,17},{1,25},{10,2},{18... | collective-permute-start | bytes 29192 | tf_op jit(solution)/shard_map/ppermute | solution.py:73
  116.7 19.2 %collective-permute-start.4 = (f32[19,16,8,1]{0,2,3,1:T(8,128)S(1)}, f32[19,16,8,1]{0,2,3,1:T(8,128)S(1)}, u32[]{:S(2)}, u32[]{:S(2)}) collective-permute-start(f32[19,16,8,1]{0,2,3,1:T(8,128)S(1)} %copy.45), channel_id=1, source_target_pairs={{0,8},{8,16},{16,24},{24,0},{1,9},{9,17},{17,25},{25,1},{2,10},{10... | collective-permute-start | bytes 29192 | tf_op jit(solution)/shard_map/ppermute | solution.py:72
  146.2 9.6 %collective-permute-start.6 = (f32[19,16,1,130]{3,2,1,0:T(1,128)S(1)}, f32[19,16,1,130]{3,2,1,0:T(1,128)S(1)}, u32[]{:S(2)}, u32[]{:S(2)}) collective-permute-start(f32[19,16,1,130]{3,2,1,0:T(1,128)S(1)} %get-tuple-element.62), channel_id=1, source_target_pairs={{0,1},{1,2},{2,3},{3,4},{4,5},{5,6},{6,7},{7,0},{8,9},{9,10},{10,1... | collective-permute-start | bytes 474248 | tf_op jit(solution)/shard_map/ppermute | solution.py:72
  146.2 10.3 %collective-permute-start.7 = (f32[19,16,1,130]{3,2,1,0:T(1,128)S(1)}, f32[19,16,1,130]{3,2,1,0:T(1,128)S(1)}, u32[]{:S(2)}, u32[]{:S(2)}) collective-permute-start(f32[19,16,1,130]{3,2,1,0:T(1,128)S(1)} %get-tuple-element.61), channel_id=1, source_target_pairs={{1,0},{2,1},{3,2},{4,3},{5,4},{6,5},{7,6},{0,7},{9,8},{10,9},{11,1... | collective-permute-start | bytes 474248 | tf_op jit(solution)/shard_map/ppermute | solution.py:73
  164.5 14.3 %copy-start.74 = (f32[5]{0:T(128)S(1)}, f32[5]{0:T(128)}, u32[]{:S(2)}) copy-start(f32[5]{0:T(128)} %constant.146) | copy-start | bytes 64
  165.3 13.8 %copy-start.73 = (f32[5]{0:T(128)S(1)}, f32[5]{0:T(128)}, u32[]{:S(2)}) copy-start(f32[5]{0:T(128)} %constant.144) | copy-start | bytes 64
  169.6 9.6 %copy-start.46 = (f32[15,8,128]{2,1,0:T(8,128)S(1)}, f32[15,8,128]{2,1,0:T(8,128)}, u32[]{:S(2)}) copy-start(f32[15,8,128]{2,1,0:T(8,128)} %get-tuple-element.78) | copy-start | bytes 184324
  169.6 10.2 %copy-start.1 = (f32[19,16,8,1]{3,2,1,0:T(8,128)S(1)}, f32[19,16,8,1]{3,2,1,0:T(8,128)}, u32[]{:S(2)}) copy-start(f32[19,16,8,1]{3,2,1,0:T(8,128)} %copy.46) | copy-start | bytes 29188
  179.8 2.1 %copy-start.45 = (f32[15,8,128]{2,1,0:T(8,128)S(1)}, f32[15,8,128]{2,1,0:T(8,128)}, u32[]{:S(2)}) copy-start(f32[15,8,128]{2,1,0:T(8,128)} %get-tuple-element.77) | copy-start | bytes 184324
  179.8 2.8 %copy-start.44 = (f32[15,8,128]{2,1,0:T(8,128)S(1)}, f32[15,8,128]{2,1,0:T(8,128)}, u32[]{:S(2)}) copy-start(f32[15,8,128]{2,1,0:T(8,128)} %get-tuple-element.69) | copy-start | bytes 184324
  179.8 4.0 %copy-start.43 = (f32[15,8,128]{2,1,0:T(8,128)S(1)}, f32[15,8,128]{2,1,0:T(8,128)}, u32[]{:S(2)}) copy-start(f32[15,8,128]{2,1,0:T(8,128)} %get-tuple-element.68) | copy-start | bytes 184324
  (22 other events, 28.3 us)
where the time goes:
time: 191 us; the launch traced here: 190 us
  local copies, waits for them, and re-layouts  63.7 us (33%)
  other arithmetic  54.5 us (29%)
  blocking collectives  35.1 us (18%)
  starting transfers between devices  13.1 us (7%)
  waiting for transfers between devices  10.1 us (5%)
  between operations  8.13 us (4%)
  matrix products  4.87 us (3%)
    unnamed x44, other arithmetic  25.5 us
    unnamed x179, local copies, waits for them, and re-layouts  20.6 us
    all_gather x2, blocking collectives, displaced_windows(): full = lax.all_gather(planes, 'gx', axis=3, tiled=True)  19.2 us
    psum x1, blocking collectives, local(): profiles = lax.psum(jnp.sum(accumulated, axis=3), 'gx')  16 us
    ppermute x4, waiting for transfers between devices, extended(): before = lax.ppermute(last, axis, up)  10.1 us
    ppermute x4, starting transfers between devices, extended(): after = lax.ppermute(initial, axis, down)  9.53 us
    slice x4, local copies, waits for them, and re-layouts, extended(): initial = lax.slice_in_dim(value, 0, width, axis=dim)  6.71 us
    another operation x1, local copies, waits for them, and re-layouts, assemble(): return jnp.stack(pieces)  6.33 us
  transfers between devices with their start and end apart: 8, of which 2 were waited for; matrix products, arithmetic and copies ran while one was open for 7% of the time, Pallas kernels for 0%

commit v1 on v0

--- a/solution.py
+++ b/solution.py
@@ -220,7 +220,8 @@
         le_top = (1.0 - weight) * win_top[:, :, :width_x] + weight * win_top[:, :, 1:] - top_fix
         le_bot = (1.0 - weight) * win_bot[:, :, 1:] + weight * win_bot[:, :, :width_x] + bot_fix
         popul = assemble(shifted, le_top, le_bot)
-    profiles = lax.psum(jnp.sum(accumulated, axis=3), "gx")
+    view = jnp.sum(accumulated, axis=3)
+    profiles = jnp.sum(lax.all_gather(view, axis_name="gx"), axis=0)
     return (popul, accumulated, profiles)
 
 

time: 191 us -> 184 us (0.963)
  blocking collectives: 35.1 us -> 28.5 us
    psum x1 -> x0, blocking collectives: 16 us -> none  [local(): profiles = lax.psum(jnp.sum(accumulated, axis=3), 'gx')]
    all_gather x0 -> x1, blocking collectives: none -> 8.42 us  [local(): profiles = jnp.sum(lax.all_gather(view, axis_name='gx'), axis=0)]
    unnamed x179 -> x178, local copies, waits for them, and re-layouts: 20.6 us -> 20 us
where the time goes in v1:
time: 184 us; the launch traced here: 183 us
  local copies, waits for them, and re-layouts  63.1 us (34%)
  other arithmetic  55.1 us (30%)
  blocking collectives  28.5 us (15%)
  starting transfers between devices  13.1 us (7%)
  waiting for transfers between devices  10.1 us (5%)
  between operations  8.13 us (4%)
  matrix products  4.87 us (3%)
    unnamed x44, other arithmetic  25.5 us
    all_gather x2, blocking collectives, displaced_windows(): full = lax.all_gather(planes, 'gx', axis=3, tiled=True)  20.1 us
    unnamed x178, local copies, waits for them, and re-layouts  20 us
    ppermute x4, waiting for transfers between devices, extended(): before = lax.ppermute(last, axis, up)  10.1 us
    ppermute x4, starting transfers between devices, extended(): after = lax.ppermute(initial, axis, down)  9.53 us
    all_gather x1, blocking collectives, local(): profiles = jnp.sum(lax.all_gather(view, axis_name='gx'), axis=0)  8.42 us
    slice x4, local copies, waits for them, and re-layouts, extended(): initial = lax.slice_in_dim(value, 0, width, axis=dim)  6.71 us
    another operation x1, local copies, waits for them, and re-layouts, assemble(): return jnp.stack(pieces)  6.33 us
  transfers between devices with their start and end apart: 8, of which 2 were waited for; matrix products, arithmetic and copies ran while one was open for 7% of the time, Pallas kernels for 0%

profile of v1, /device:TPU:0, one launch (start us, length us, event | category | flops | bytes accessed | tf_op | source)
XLA Modules:
  0.0 182.9 jit_solution(4255828108452994812)
XLA Ops:
  0.7 0.8 pad_clamp_fusion
  1.5 1.9 %multiply_reduce_fusion.6 = (f32[16,8,128]{2,1,0:T(8,128)S(1)}, f32[16,8,128]{2,1,0:T(8,128)S(1)}, f32[16,8,128]{2,1,0:T(8,128)S(1)}, f32[16,8,128]{2,1,0:T(8,128)S(1)}) fusion(f32[19]{0:T(128)} %constant.136, f32[19,16,8,128]{3,2,1,0:T(8,128)} %param.36, f32[19]{0:T(128)} %constant.134, f32[19]{0:T(128)} %constant.137, f32[19]{0:T(128)} %constant.138), kind=kLoop, calls=%fused_computation.42 | loop fusion | flops 2424832 | bytes 1507632 | tf_op jit(solution)/shard_map/reduce_sum | solution.py:131
  4.0 2.2 %fusion.17 = (f32[19,16,8,128]{3,2,1,0:T(8,128)S(1)}, f32[19,16,8,128]{3,2,1,0:T(8,128)}) fusion(f32[16,8,128]{2,1,0:T(8,128)S(1)} %get-tuple-element.44, f32[16,8,128]{2,1,0:T(8,128)S(1)} %get-tuple-element.47, f32[19]{0:T(128)S(1)} %copy-done.68, f32[16,8,128]{2,1,0:T(8,128)S(1)} %get-tuple-element.46, f32[19]{0:T(128)S(1)} %copy-done.65, ...), kind=kLoop, calls=%fused_computation.25 | loop fusion | flops 4669440 | bytes 4063536 | tf_op jit(solution)/shard_map/sub | solution.py:147
  6.4 0.9 copy-done.8
  7.3 0.9 copy.64
  8.2 1.4 fusion.92
  9.6 1.4 copy.65
  11.3 1.8 gt.9
  13.1 1.7 gather_fusion
  14.8 1.9 %fusion.25 = f32[19,16,8,128]{3,2,1,0:T(8,128)S(1)} fusion(f32[19,16,8,128]{3,2,1,0:T(8,128)} %gather_fusion, f32[24,128,128]{2,1,0:T(8,128)} %bitcast.263, pred[16,8,128]{2,1,0:T(8,128)(4,1)S(1)} %gt.9, f32[19,16,8,128]{3,2,1,0:T(8,128)S(1)} %copy-done.7, f32[19]{0:T(128)S(1)} %copy-done.63), kind=kLoop, calls=%fused_computation.35 | loop fusion | flops 933888 | bytes 4997196 | tf_op jit(solution)/shard_map/jit(_where)/select_n | solution.py:151
  16.6 1.5 fusion.85
  18.1 2.2 %copy.51 = f32[19,16,8,1]{0,2,3,1:T(8,128)S(1)} copy(f32[19,16,8,1]{3,2,1,0:T(8,128)} %get-tuple-element.87) | data formatting | bytes 19456 | tf_op jit(solution)/shard_map/slice | solution.py:70
  20.3 3.0 %collective-permute-start = (f32[19,16,8,1]{0,2,3,1:T(8,128)S(1)}, f32[19,16,8,1]{0,2,3,1:T(8,128)S(1)}, u32[]{:S(2)}, u32[]{:S(2)}) collective-permute-start(f32[19,16,8,1]{0,2,3,1:T(8,128)S(1)} %copy.51), channel_id=1, source_target_pairs={{0,8},{8,16},{16,24},{24,0},{1,9},{9,17},{17,25},{25,1},{2,10},{10... | collective-permute-start | bytes 29192 | tf_op jit(solution)/shard_map/ppermute | solution.py:72
  23.3 1.6 copy.53
  24.9 1.0 collective-permute-start.1
  33.8 2.3 %sub.117 = f32[1,16,8,128]{3,2,1,0:T(8,128)} reshape(f32[4,4,2,4,32,4]{5,4,3,2,1,0:T(8,128)S(1)} %broadcast_in_dim.49) | data formatting | bytes 131072 | tf_op jit(solution)/shard_map/sub | solution.py:152
  36.7 1.3 copy.52
  38.0 3.1 %copy.54 = f32[19,16,8,1]{3,2,1,0:T(8,128)} copy(f32[19,16,8,1]{0,2,3,1:T(8,128)} %collective-permute-done.1) | data formatting | bytes 19456 | tf_op jit(solution)/shard_map/ppermute | solution.py:73
  41.1 1.8 fusion.50
  42.8 2.0 %pad_maximum_fusion.3 = (f32[19,16,1,130]{3,2,1,0:T(1,128)S(1)}, f32[19,16,1,130]{3,2,1,0:T(1,128)S(1)}) fusion(f32[19,16,8,1]{3,2,1,0:T(8,128)S(1)} %copy-done.2, f32[19,16,8,128]{3,2,1,0:T(8,128)S(1)} %fusion.25, f32[19,16,8,1]{3,2,1,0:T(8,128)S(1)} %copy.52), kind=kLoop, calls=%fused_computation.59 | loop fusion | flops 158080 | bytes 1580800 | tf_op jit(solution)/shard_map/concatenate | solution.py:74
  44.8 0.7 constant_dynamic-update-slice_fusion.34
  45.6 0.8 constant_dynamic-update-slice_fusion.33
  46.3 2.5 %copy.83 = f32[19,16,8,128]{3,2,1,0:T(8,128)} copy(f32[19,16,8,128]{3,2,1,0:T(8,128)} %get-tuple-element.40) | data formatting | bytes 2490368
  48.8 3.5 %collective-permute-start.3 = (f32[19,16,1,130]{3,2,1,0:T(1,128)S(1)}, f32[19,16,1,130]{3,2,1,0:T(1,128)S(1)}, u32[]{:S(2)}, u32[]{:S(2)}) collective-permute-start(f32[19,16,1,130]{3,2,1,0:T(1,128)S(1)} %get-tuple-element.62), channel_id=1, source_target_pairs={{1,0},{2,1},{3,2},{4,3},{5,4},{6,5},{7,6},{0,7},{9,8},{10,9},{11,1... | collective-permute-start | bytes 474248 | tf_op jit(solution)/shard_map/ppermute | solution.py:73
  53.0 4.7 %collective-permute-done.2 = f32[19,16,1,130]{3,2,1,0:T(1,128)S(1)} collective-permute-done((f32[19,16,1,130]{3,2,1,0:T(1,128)S(1)}, f32[19,16,1,130]{3,2,1,0:T(1,128)S(1)}, u32[]{:S(2)}, u32[]{:S(2)}) %collective-permute-start.2) | collective-permute-done | bytes 158112 | tf_op jit(solution)/shard_map/ppermute | solution.py:72
  58.4 0.7 constant_dynamic-update-slice_fusion.11
  62.8 0.8 constant_dynamic-update-slice_fusion.5
  64.3 0.8 constant_dynamic-update-slice_fusion.3
  65.8 0.8 constant_dynamic-update-slice_fusion.1
  67.3 1.9 %gather_fusion.2 = f32[5,8,128]{2,1,0:T(8,128)S(1)} fusion(f32[19,16,8,128]{3,2,1,0:T(8,128)} %constant_dynamic-update-slice_fusion, s32[5]{0:T(128)S(1)} %copy-done.48), kind=kCustom, calls=%fused_computation.2 | custom fusion | bytes 41000 | tf_op jit(solution)/shard_map/gather | solution.py:218
  69.2 2.5 %gather_fusion.1 = f32[5,8,128]{2,1,0:T(8,128)} fusion(f32[19,16,8,128]{3,2,1,0:T(8,128)} %constant_dynamic-update-slice_fusion, s32[5]{0:T(128)S(1)} %copy-done.47), kind=kCustom, calls=%fused_computation.1 | custom fusion | bytes 41000 | tf_op jit(solution)/shard_map/gather | solution.py:218
  71.7 0.8 pad_maximum_fusion.48
  72.5 10.9 %all_gather.12 = f32[2,5,8,512]{3,2,1,0:T(8,128)S(1)} all-gather(f32[2,5,8,128]{3,2,1,0:T(8,128)S(1)} %pad_maximum_fusion.48), channel_id=1, replica_groups=mesh['gx'=4,'gz'=8] {'gx'}, dimensions={3}, use_global_device_ids=true | all-gather | bytes 204800 | tf_op jit(solution)/shard_map/all_gather | solution.py:194
  85.6 1.1 copy-done.4
  87.0 1.0 copy-done.5
  88.0 1.0 multiply_reduce_fusion.1
  89.1 2.2 %gather_fusion.3 = f32[19,16,8,128]{3,2,1,0:T(8,128)S(1)} fusion(f32[19,16,8,128]{3,2,1,0:T(8,128)} %copy-done.5, s32[1024]{0:T(1024)} %copy-done.71), kind=kCustom, calls=%fused_computation.3 | custom fusion | bytes 2490444 | tf_op jit(solution)/shard_map/gather | solution.py:151
  92.1 1.4 pad_maximum_fusion.23
  93.5 1.3 pad_maximum_fusion.25
  96.2 0.8 fusion.69
  97.7 6.3 %stack.178 = f32[19,16384]{1,0:T(8,128)} concatenate(f32[1,16384]{1,0:T(1,128)} %bitcast.277, f32[1,16384]{1,0:T(1,128)} %bitcast.273, f32[1,16384]{1,0:T(1,128)} %bitcast.274, f32[1,16384]{1,0:T(1,128)} %bitcast.278, f32[1,16384]{1,0:T(1,128)} %bitcast.280, f32[1,16384]{1,0:T(1,128)S(1)} %bitcast.265, f32[1,16384]{1,0:T(1,128)S(1)} %bitcast.266, f32[1,16384]{1,0:T(1,128)} %bitcast.279, ...), dimensions={0} | concatenate | bytes 2490368 | tf_op jit(solution)/shard_map/stack | solution.py:173
  104.1 3.5 %fusion.4 = f32[19,16384]{1,0:T(8,128)S(1)} fusion(f32[19,19]{1,0:T(8,128)S(1)} %copy-done.59, f32[19,16384]{1,0:T(8,128)} %stack.178, f32[16384]{0:T(1024)S(1)} %bitcast.275, f32[16384]{0:T(1024)S(1)} %get-tuple-element.90, f32[19]{0:T(128)S(1)} %copy-done.70, f32[16384]{0:T(1024)S(1)} %get-tuple-element.93, f32[19]{0:T(128)S(1)} %copy-done.67, ...), kind=kOutput, calls=%fused_computation.13 | convolution fusion | flops 75333632 | bytes 2819796 | tf_op jit(solution)/shard_map/dot_general | solution.py:148
  107.9 1.0 copy-done.6
  109.2 1.3 fusion.23
  110.5 1.5 fusion.83
  112.0 2.2 %copy.59 = f32[19,16,8,1]{0,2,3,1:T(8,128)S(1)} copy(f32[19,16,8,1]{3,2,1,0:T(8,128)} %get-tuple-element.79) | data formatting | bytes 19456 | tf_op jit(solution)/shard_map/slice | solution.py:71
  114.2 1.5 collective-permute-start.5
  115.7 1.0 copy.57
  118.0 8.4 %all-gather = f32[8,16,8]{1,2,0:T(8,128)S(1)} all-gather(f32[2,16,8]{1,2,0:T(8,128)S(1)} %copy.63), channel_id=2, replica_groups=mesh['gx'=4,'gz'=8] {'gx'}, dimensions={0}, use_global_device_ids=true | all-gather | bytes 5120 | tf_op jit(solution)/shard_map/all_gather | solution.py:224
  127.0 1.3 copy.60
  128.3 2.2 %copy.58 = f32[19,16,8,1]{3,2,1,0:T(8,128)} copy(f32[19,16,8,1]{0,2,3,1:T(8,128)S(1)} %collective-permute-done.4) | data formatting | bytes 19456 | tf_op jit(solution)/shard_map/ppermute | solution.py:72
  130.6 1.6 pad_maximum_fusion.12
  132.2 0.8 fusion.46
  133.0 2.0 %pad_maximum_fusion = (f32[19,16,1,130]{3,2,1,0:T(1,128)S(1)}, f32[19,16,1,130]{3,2,1,0:T(1,128)S(1)}) fusion(f32[19,16,8,1]{3,2,1,0:T(8,128)S(1)} %copy.60, f32[19,16,8,128]{3,2,1,0:T(8,128)S(1)} %get-tuple-element.72, f32[19,16,8,1]{3,2,1,0:T(8,128)S(1)} %copy-done), kind=kLoop, calls=%fused_computation.56 | loop fusion | flops 158080 | bytes 1580800 | tf_op jit(solution)/shard_map/concatenate | solution.py:74
  136.2 2.4 %copy.115 = f32[19,16,8,128]{3,2,1,0:T(8,128)} copy(f32[19,16,8,128]{3,2,1,0:T(8,128)} %constant_dynamic-update-slice_fusion.69) | data formatting | bytes 2490368
  138.7 3.5 %collective-permute-start.7 = (f32[19,16,1,130]{3,2,1,0:T(1,128)S(1)}, f32[19,16,1,130]{3,2,1,0:T(1,128)S(1)}, u32[]{:S(2)}, u32[]{:S(2)}) collective-permute-start(f32[19,16,1,130]{3,2,1,0:T(1,128)S(1)} %get-tuple-element.58), channel_id=1, source_target_pairs={{1,0},{2,1},{3,2},{4,3},{5,4},{6,5},{7,6},{0,7},{9,8},{10,9},{11,1... | collective-permute-start | bytes 474248 | tf_op jit(solution)/shard_map/ppermute | solution.py:73
  142.9 5.4 %collective-permute-done.6 = f32[19,16,1,130]{3,2,1,0:T(1,128)S(1)} collective-permute-done((f32[19,16,1,130]{3,2,1,0:T(1,128)S(1)}, f32[19,16,1,130]{3,2,1,0:T(1,128)S(1)}, u32[]{:S(2)}, u32[]{:S(2)}) %collective-permute-start.6) | collective-permute-done | bytes 158112 | tf_op jit(solution)/shard_map/ppermute | solution.py:72
  153.3 0.7 constant_dynamic-update-slice_fusion.41
  154.7 0.8 constant_dynamic-update-slice_fusion.39
  156.2 0.8 constant_dynamic-update-slice_fusion.37
  157.7 1.9 %gather_fusion.5 = f32[5,8,128]{2,1,0:T(8,128)S(1)} fusion(f32[19,16,8,128]{3,2,1,0:T(8,128)} %constant_dynamic-update-slice_fusion.36, s32[5]{0:T(128)S(1)} %copy-done.48), kind=kCustom, calls=%fused_computation.5 | custom fusion | bytes 41000 | tf_op jit(solution)/shard_map/gather | solution.py:218
  159.6 2.5 %gather_fusion.4 = f32[5,8,128]{2,1,0:T(8,128)} fusion(f32[19,16,8,128]{3,2,1,0:T(8,128)} %constant_dynamic-update-slice_fusion.36, s32[5]{0:T(128)S(1)} %copy-done.47), kind=kCustom, calls=%fused_computation.4 | custom fusion | bytes 41000 | tf_op jit(solution)/shard_map/gather | solution.py:218
  162.1 0.8 pad_maximum_fusion.49
  162.9 9.1 %all_gather.13 = f32[2,5,8,512]{3,2,1,0:T(8,128)S(1)} all-gather(f32[2,5,8,128]{3,2,1,0:T(8,128)S(1)} %pad_maximum_fusion.49), channel_id=1, replica_groups=mesh['gx'=4,'gz'=8] {'gx'}, dimensions={3}, use_global_device_ids=true | all-gather | bytes 204800 | tf_op jit(solution)/shard_map/all_gather | solution.py:194
  (254 shorter events, 37.7 us)
Async XLA Ops:
  0.6 3.4 %copy-start.60 = (f32[19]{0:T(128)S(1)}, f32[19]{0:T(128)}, u32[]{:S(2)}) copy-start(f32[19]{0:T(128)} %constant.136) | copy-start | bytes 232
  0.6 3.4 %copy-start.63 = (f32[19]{0:T(128)S(1)}, f32[19]{0:T(128)}, u32[]{:S(2)}) copy-start(f32[19]{0:T(128)} %constant.134) | copy-start | bytes 232
  0.7 3.4 %copy-start.65 = (f32[19]{0:T(128)S(1)}, f32[19]{0:T(128)}, u32[]{:S(2)}) copy-start(f32[19]{0:T(128)} %constant.137) | copy-start | bytes 232
  0.7 3.4 %copy-start.68 = (f32[19]{0:T(128)S(1)}, f32[19]{0:T(128)}, u32[]{:S(2)}) copy-start(f32[19]{0:T(128)} %constant.138) | copy-start | bytes 232
  0.7 3.3 %copy-start.7 = (f32[19,16,8,128]{3,2,1,0:T(8,128)S(1)}, f32[19,16,8,128]{3,2,1,0:T(8,128)}, u32[]{:S(2)}) copy-start(f32[19,16,8,128]{3,2,1,0:T(8,128)} %param.36) | copy-start | bytes 3735556
  1.5 11.6 %copy-start.71 = (s32[1024]{0:T(1024)}, s32[1024]{0:T(1024)S(1)}, u32[]{:S(2)}) copy-start(s32[1024]{0:T(1024)S(1)} %pad_clamp_fusion) | copy-start | bytes 12292
  9.6 3.5 %copy-start.10 = (f32[19,16,8,128]{3,2,1,0:T(8,128)S(1)}, f32[19,16,8,128]{3,2,1,0:T(8,128)}, u32[]{:S(2)}) copy-start(f32[19,16,8,128]{3,2,1,0:T(8,128)} %get-tuple-element.71) | copy-start | bytes 3735556
  18.1 8.4 %copy-start.75 = (s32[2]{0:T(128)S(1)}, s32[2]{0:T(128)}, u32[]{:S(2)}) copy-start(s32[2]{0:T(128)} %param.38) | copy-start | bytes 28
  18.1 9.0 %copy-start.76 = (s32[2]{0:T(128)S(1)}, s32[2]{0:T(128)}, u32[]{:S(2)}) copy-start(s32[2]{0:T(128)} %param.39) | copy-start | bytes 28
  20.3 16.4 %collective-permute-start = (f32[19,16,8,1]{0,2,3,1:T(8,128)S(1)}, f32[19,16,8,1]{0,2,3,1:T(8,128)S(1)}, u32[]{:S(2)}, u32[]{:S(2)}) collective-permute-start(f32[19,16,8,1]{0,2,3,1:T(8,128)S(1)} %copy.51), channel_id=1, source_target_pairs={{0,8},{8,16},{16,24},{24,0},{1,9},{9,17},{17,25},{25,1},{2,10},{10... | collective-permute-start | bytes 29192 | tf_op jit(solution)/shard_map/ppermute | solution.py:72
  24.9 13.1 %collective-permute-start.1 = (f32[19,16,8,1]{0,2,3,1:T(8,128)}, f32[19,16,8,1]{0,2,3,1:T(8,128)}, u32[]{:S(2)}, u32[]{:S(2)}) collective-permute-start(f32[19,16,8,1]{0,2,3,1:T(8,128)} %copy.53), channel_id=1, source_target_pairs={{8,0},{16,8},{24,16},{0,24},{9,1},{17,9},{25,17},{1,25},{10,2},{18... | collective-permute-start | bytes 29192 | tf_op jit(solution)/shard_map/ppermute | solution.py:73
  41.1 1.8 copy-start.2
  48.8 8.9 %collective-permute-start.2 = (f32[19,16,1,130]{3,2,1,0:T(1,128)S(1)}, f32[19,16,1,130]{3,2,1,0:T(1,128)S(1)}, u32[]{:S(2)}, u32[]{:S(2)}) collective-permute-start(f32[19,16,1,130]{3,2,1,0:T(1,128)S(1)} %get-tuple-element.63), channel_id=1, source_target_pairs={{0,1},{1,2},{2,3},{3,4},{4,5},{5,6},{6,7},{7,0},{8,9},{9,10},{10,1... | collective-permute-start | bytes 474248 | tf_op jit(solution)/shard_map/ppermute | solution.py:72
  48.8 9.6 %collective-permute-start.3 = (f32[19,16,1,130]{3,2,1,0:T(1,128)S(1)}, f32[19,16,1,130]{3,2,1,0:T(1,128)S(1)}, u32[]{:S(2)}, u32[]{:S(2)}) collective-permute-start(f32[19,16,1,130]{3,2,1,0:T(1,128)S(1)} %get-tuple-element.62), channel_id=1, source_target_pairs={{1,0},{2,1},{3,2},{4,3},{5,4},{6,5},{7,6},{0,7},{9,8},{10,9},{11,1... | collective-permute-start | bytes 474248 | tf_op jit(solution)/shard_map/ppermute | solution.py:73
  66.6 2.6 %copy-start.47 = (s32[5]{0:T(128)S(1)}, s32[5]{0:T(128)}, u32[]{:S(2)}) copy-start(s32[5]{0:T(128)} %constant.208) | copy-start | bytes 64
  67.3 17.1 %copy-start.72 = (f32[5]{0:T(128)S(1)}, f32[5]{0:T(128)}, u32[]{:S(2)}) copy-start(f32[5]{0:T(128)} %constant.144) | copy-start | bytes 64
  71.7 12.9 %copy-start.17 = (f32[15,8,128]{2,1,0:T(8,128)S(1)}, f32[15,8,128]{2,1,0:T(8,128)}, u32[]{:S(2)}) copy-start(f32[15,8,128]{2,1,0:T(8,128)} %get-tuple-element.85) | copy-start | bytes 184324
  71.7 13.5 %copy-start.3 = (f32[19,16,8,1]{3,2,1,0:T(8,128)S(1)}, f32[19,16,8,1]{3,2,1,0:T(8,128)}, u32[]{:S(2)}) copy-start(f32[19,16,8,1]{3,2,1,0:T(8,128)} %copy.54) | copy-start | bytes 29188
  84.6 2.2 %copy-start.53 = (f32[1,8,128]{2,1,0:T(8,128)}, f32[1,8,128]{2,1,0:T(8,128)S(1)}, u32[]{:S(2)}) copy-start(f32[1,8,128]{2,1,0:T(8,128)S(1)} %get-tuple-element.111) | copy-start | bytes 12292
  84.6 2.2 %copy-start.51 = (f32[1,8,128]{2,1,0:T(8,128)}, f32[1,8,128]{2,1,0:T(8,128)S(1)}, u32[]{:S(2)}) copy-start(f32[1,8,128]{2,1,0:T(8,128)S(1)} %get-tuple-element.110) | copy-start | bytes 12292
  84.6 2.3 %copy-start.49 = (f32[1,8,128]{2,1,0:T(8,128)}, f32[1,8,128]{2,1,0:T(8,128)S(1)}, u32[]{:S(2)}) copy-start(f32[1,8,128]{2,1,0:T(8,128)S(1)} %get-tuple-element.109) | copy-start | bytes 12292
  85.5 2.5 %copy-start.61 = (f32[19]{0:T(128)S(1)}, f32[19]{0:T(128)}, u32[]{:S(2)}) copy-start(f32[19]{0:T(128)} %constant.136) | copy-start | bytes 232
  85.5 2.5 %copy-start.66 = (f32[19]{0:T(128)S(1)}, f32[19]{0:T(128)}, u32[]{:S(2)}) copy-start(f32[19]{0:T(128)} %constant.137) | copy-start | bytes 232
  85.5 2.5 %copy-start.69 = (f32[19]{0:T(128)S(1)}, f32[19]{0:T(128)}, u32[]{:S(2)}) copy-start(f32[19]{0:T(128)} %constant.138) | copy-start | bytes 232
  89.0 2.3 %copy-start.16 = (f32[15,8,128]{2,1,0:T(8,128)S(1)}, f32[15,8,128]{2,1,0:T(8,128)}, u32[]{:S(2)}) copy-start(f32[15,8,128]{2,1,0:T(8,128)} %get-tuple-element.84) | copy-start | bytes 184324
  89.0 2.3 %copy-start.18 = (f32[15,8,128]{2,1,0:T(8,128)S(1)}, f32[15,8,128]{2,1,0:T(8,128)}, u32[]{:S(2)}) copy-start(f32[15,8,128]{2,1,0:T(8,128)} %get-tuple-element.85) | copy-start | bytes 184324
  89.0 3.0 %copy-start.28 = (f32[15,8,128]{2,1,0:T(8,128)S(1)}, f32[15,8,128]{2,1,0:T(8,128)}, u32[]{:S(2)}) copy-start(f32[15,8,128]{2,1,0:T(8,128)} %copy-done.27) | copy-start | bytes 184324
  89.1 3.0 %copy-start.30 = (f32[15,8,128]{2,1,0:T(8,128)S(1)}, f32[15,8,128]{2,1,0:T(8,128)}, u32[]{:S(2)}) copy-start(f32[15,8,128]{2,1,0:T(8,128)} %copy-done.29) | copy-start | bytes 184324
  89.1 3.0 %copy-start.52 = (f32[1,8,128]{2,1,0:T(8,128)S(1)}, f32[1,8,128]{2,1,0:T(8,128)}, u32[]{:S(2)}) copy-start(f32[1,8,128]{2,1,0:T(8,128)} %copy-done.51) | copy-start | bytes 12292
  89.1 4.4 %copy-start.12 = (f32[15,8,128]{2,1,0:T(8,128)S(1)}, f32[15,8,128]{2,1,0:T(8,128)}, u32[]{:S(2)}) copy-start(f32[15,8,128]{2,1,0:T(8,128)} %get-tuple-element.68) | copy-start | bytes 184324
  89.1 4.4 %copy-start.14 = (f32[15,8,128]{2,1,0:T(8,128)S(1)}, f32[15,8,128]{2,1,0:T(8,128)}, u32[]{:S(2)}) copy-start(f32[15,8,128]{2,1,0:T(8,128)} %get-tuple-element.69) | copy-start | bytes 184324
  89.1 5.7 %copy-start.22 = (f32[15,8,128]{2,1,0:T(8,128)S(1)}, f32[15,8,128]{2,1,0:T(8,128)}, u32[]{:S(2)}) copy-start(f32[15,8,128]{2,1,0:T(8,128)} %copy-done.21) | copy-start | bytes 184324
  89.1 5.7 %copy-start.26 = (f32[15,8,128]{2,1,0:T(8,128)S(1)}, f32[15,8,128]{2,1,0:T(8,128)}, u32[]{:S(2)}) copy-start(f32[15,8,128]{2,1,0:T(8,128)} %copy-done.25) | copy-start | bytes 184324
  89.1 6.4 %copy-start.20 = (f32[15,8,128]{2,1,0:T(8,128)S(1)}, f32[15,8,128]{2,1,0:T(8,128)}, u32[]{:S(2)}) copy-start(f32[15,8,128]{2,1,0:T(8,128)} %copy-done.19) | copy-start | bytes 184324
  89.1 6.4 %copy-start.24 = (f32[15,8,128]{2,1,0:T(8,128)S(1)}, f32[15,8,128]{2,1,0:T(8,128)}, u32[]{:S(2)}) copy-start(f32[15,8,128]{2,1,0:T(8,128)} %copy-done.23) | copy-start | bytes 184324
  89.1 6.4 %copy-start.50 = (f32[1,8,128]{2,1,0:T(8,128)S(1)}, f32[1,8,128]{2,1,0:T(8,128)}, u32[]{:S(2)}) copy-start(f32[1,8,128]{2,1,0:T(8,128)} %copy-done.49) | copy-start | bytes 12292
  91.3 4.8 %copy-start.35 = (f32[16,8,128]{2,1,0:T(8,128)S(1)}, f32[16,8,128]{2,1,0:T(8,128)}, u32[]{:S(2)}) copy-start(f32[16,8,128]{2,1,0:T(8,128)} %get-tuple-element.9) | copy-start | bytes 196612
  91.3 4.8 %copy-start.38 = (f32[1,16,8,128]{3,2,1,0:T(8,128)S(1)}, f32[1,16,8,128]{3,2,1,0:T(8,128)}, u32[]{:S(2)}) copy-start(f32[1,16,8,128]{3,2,1,0:T(8,128)} %get-tuple-element.43) | copy-start | bytes 196612
  91.3 4.8 %copy-start.39 = (f32[1,16,8,128]{3,2,1,0:T(8,128)S(1)}, f32[1,16,8,128]{3,2,1,0:T(8,128)}, u32[]{:S(2)}) copy-start(f32[1,16,8,128]{3,2,1,0:T(8,128)} %get-tuple-element.41) | copy-start | bytes 196612
  91.4 4.8 %copy-start.54 = (f32[1,8,128]{2,1,0:T(8,128)S(1)}, f32[1,8,128]{2,1,0:T(8,128)}, u32[]{:S(2)}) copy-start(f32[1,8,128]{2,1,0:T(8,128)} %copy-done.53) | copy-start | bytes 12292
  91.4 4.8 %copy-start.56 = (f32[1,8,128]{2,1,0:T(8,128)S(1)}, f32[1,8,128]{2,1,0:T(8,128)}, u32[]{:S(2)}) copy-start(f32[1,8,128]{2,1,0:T(8,128)} %copy-done.55) | copy-start | bytes 12292
  92.0 5.5 %copy-start.33 = (f32[1,16,8,128]{3,2,1,0:T(8,128)S(1)}, f32[1,16,8,128]{3,2,1,0:T(8,128)}, u32[]{:S(2)}) copy-start(f32[1,16,8,128]{3,2,1,0:T(8,128)} %sub.117) | copy-start | bytes 196612
  92.1 5.5 %copy-start.37 = (f32[16,8,128]{2,1,0:T(8,128)S(1)}, f32[16,8,128]{2,1,0:T(8,128)}, u32[]{:S(2)}) copy-start(f32[16,8,128]{2,1,0:T(8,128)} %copy-done.36) | copy-start | bytes 196612
  92.1 5.5 %copy-start.41 = (f32[16,8,128]{2,1,0:T(8,128)S(1)}, f32[16,8,128]{2,1,0:T(8,128)}, u32[]{:S(2)}) copy-start(f32[16,8,128]{2,1,0:T(8,128)} %get-tuple-element.7) | copy-start | bytes 196612
  92.1 5.5 %copy-start.42 = (f32[16,8,128]{2,1,0:T(8,128)S(1)}, f32[16,8,128]{2,1,0:T(8,128)}, u32[]{:S(2)}) copy-start(f32[16,8,128]{2,1,0:T(8,128)} %get-tuple-element.8) | copy-start | bytes 196612
  97.6 6.4 %copy-start.32 = (f32[1,16,8,128]{3,2,1,0:T(8,128)S(1)}, f32[1,16,8,128]{3,2,1,0:T(8,128)}, u32[]{:S(2)}) copy-start(f32[1,16,8,128]{3,2,1,0:T(8,128)} %copy-done.31) | copy-start | bytes 196612
  97.6 6.4 %copy-start.59 = (f32[19,19]{1,0:T(8,128)S(1)}, f32[19,19]{1,0:T(8,128)}, u32[]{:S(2)}) copy-start(f32[19,19]{1,0:T(8,128)} %constant.119.clone) | copy-start | bytes 4336
  97.6 6.4 %copy-start.62 = (f32[19]{0:T(128)S(1)}, f32[19]{0:T(128)}, u32[]{:S(2)}) copy-start(f32[19]{0:T(128)} %constant.136) | copy-start | bytes 232
  97.6 6.4 %copy-start.64 = (f32[19]{0:T(128)S(1)}, f32[19]{0:T(128)}, u32[]{:S(2)}) copy-start(f32[19]{0:T(128)} %constant.134) | copy-start | bytes 232
  97.7 6.4 %copy-start.67 = (f32[19]{0:T(128)S(1)}, f32[19]{0:T(128)}, u32[]{:S(2)}) copy-start(f32[19]{0:T(128)} %constant.137) | copy-start | bytes 232
  97.7 6.4 %copy-start.70 = (f32[19]{0:T(128)S(1)}, f32[19]{0:T(128)}, u32[]{:S(2)}) copy-start(f32[19]{0:T(128)} %constant.138) | copy-start | bytes 232
  107.6 1.7 copy-start.9
  112.0 5.2 %copy-start.34 = (f32[1,16,8,128]{3,2,1,0:T(8,128)S(1)}, f32[1,16,8,128]{3,2,1,0:T(8,128)}, u32[]{:S(2)}) copy-start(f32[1,16,8,128]{3,2,1,0:T(8,128)} %sub.117) | copy-start | bytes 196612
  114.2 12.8 %collective-permute-start.5 = (f32[19,16,8,1]{0,2,3,1:T(8,128)S(1)}, f32[19,16,8,1]{0,2,3,1:T(8,128)S(1)}, u32[]{:S(2)}, u32[]{:S(2)}) collective-permute-start(f32[19,16,8,1]{0,2,3,1:T(8,128)S(1)} %copy.59), channel_id=1, source_target_pairs={{8,0},{16,8},{24,16},{0,24},{9,1},{17,9},{25,17},{1,25},{10,2},{18... | collective-permute-start | bytes 29192 | tf_op jit(solution)/shard_map/ppermute | solution.py:73
  116.7 11.7 %collective-permute-start.4 = (f32[19,16,8,1]{0,2,3,1:T(8,128)S(1)}, f32[19,16,8,1]{0,2,3,1:T(8,128)S(1)}, u32[]{:S(2)}, u32[]{:S(2)}) collective-permute-start(f32[19,16,8,1]{0,2,3,1:T(8,128)S(1)} %copy.57), channel_id=1, source_target_pairs={{0,8},{8,16},{16,24},{24,0},{1,9},{9,17},{17,25},{25,1},{2,10},{10... | collective-permute-start | bytes 29192 | tf_op jit(solution)/shard_map/ppermute | solution.py:72
  138.7 9.6 %collective-permute-start.6 = (f32[19,16,1,130]{3,2,1,0:T(1,128)S(1)}, f32[19,16,1,130]{3,2,1,0:T(1,128)S(1)}, u32[]{:S(2)}, u32[]{:S(2)}) collective-permute-start(f32[19,16,1,130]{3,2,1,0:T(1,128)S(1)} %get-tuple-element.59), channel_id=1, source_target_pairs={{0,1},{1,2},{2,3},{3,4},{4,5},{5,6},{6,7},{7,0},{8,9},{9,10},{10,1... | collective-permute-start | bytes 474248 | tf_op jit(solution)/shard_map/ppermute | solution.py:72
  138.7 10.3 %collective-permute-start.7 = (f32[19,16,1,130]{3,2,1,0:T(1,128)S(1)}, f32[19,16,1,130]{3,2,1,0:T(1,128)S(1)}, u32[]{:S(2)}, u32[]{:S(2)}) collective-permute-start(f32[19,16,1,130]{3,2,1,0:T(1,128)S(1)} %get-tuple-element.58), channel_id=1, source_target_pairs={{1,0},{2,1},{3,2},{4,3},{5,4},{6,5},{7,6},{0,7},{9,8},{10,9},{11,1... | collective-permute-start | bytes 474248 | tf_op jit(solution)/shard_map/ppermute | solution.py:73
  157.0 15.2 %copy-start.74 = (f32[5]{0:T(128)S(1)}, f32[5]{0:T(128)}, u32[]{:S(2)}) copy-start(f32[5]{0:T(128)} %constant.146) | copy-start | bytes 64
  157.7 14.7 %copy-start.73 = (f32[5]{0:T(128)S(1)}, f32[5]{0:T(128)}, u32[]{:S(2)}) copy-start(f32[5]{0:T(128)} %constant.144) | copy-start | bytes 64
  162.1 10.4 %copy-start.46 = (f32[15,8,128]{2,1,0:T(8,128)S(1)}, f32[15,8,128]{2,1,0:T(8,128)}, u32[]{:S(2)}) copy-start(f32[15,8,128]{2,1,0:T(8,128)} %get-tuple-element.75) | copy-start | bytes 184324
  162.1 11.1 %copy-start.1 = (f32[19,16,8,1]{3,2,1,0:T(8,128)S(1)}, f32[19,16,8,1]{3,2,1,0:T(8,128)}, u32[]{:S(2)}) copy-start(f32[19,16,8,1]{3,2,1,0:T(8,128)} %copy.58) | copy-start | bytes 29188
  173.2 2.1 %copy-start.45 = (f32[15,8,128]{2,1,0:T(8,128)S(1)}, f32[15,8,128]{2,1,0:T(8,128)}, u32[]{:S(2)}) copy-start(f32[15,8,128]{2,1,0:T(8,128)} %get-tuple-element.74) | copy-start | bytes 184324
  173.2 2.8 %copy-start.44 = (f32[15,8,128]{2,1,0:T(8,128)S(1)}, f32[15,8,128]{2,1,0:T(8,128)}, u32[]{:S(2)}) copy-start(f32[15,8,128]{2,1,0:T(8,128)} %get-tuple-element.66) | copy-start | bytes 184324
  173.2 4.0 %copy-start.43 = (f32[15,8,128]{2,1,0:T(8,128)S(1)}, f32[15,8,128]{2,1,0:T(8,128)}, u32[]{:S(2)}) copy-start(f32[15,8,128]{2,1,0:T(8,128)} %get-tuple-element.65) | copy-start | bytes 184324
  (22 other events, 28.3 us)
